TPU v7x, 256 devices: a whole 4x4x8 slice. The times are simulated.
256 devices in a mesh: slab: 128 (over y, x, z_hi, core), grp: 2 (over z_lo).
Axes of the slice: x: 4, y: 4, z: 8 (z_hi: 4, z_lo: 2; z = z_hi * 2 + z_lo), core: 2. Of those that a mesh axis runs over, the one named last changes fastest.
Arguments:
- saturation: float32 [256, 64, 256], P(('slab', 'grp')), may hold values from 0.5 to 3
- inlet_mask: int32 [256, 64, 256], P(('slab', 'grp')), may hold values 0 or 1
- crystal_size: float32 [1048576], P(('slab', 'grp')), may hold values from 0.5 to 2
- crystal_weight: float32 [1048576], P(('slab', 'grp')), may hold values from 0.3 to 3
- crystal_cell: int32 [1048576], P(('slab', 'grp')), may hold values from 0 to 32767
- live_count: int32 [256], P(('slab', 'grp')), may hold values from 1024 to 4096, as said below
- nucleus_cell: int32 [256, 4, 512], P(('slab', 'grp')), may hold values from 0 to 32767
- nucleus_count: int32 [256, 4, 512], P(('slab', 'grp')), may hold values from 1 to 8
- migrant_rows: int32 [256, 2, 512], P(('slab', 'grp')), may hold values from 0 to 4095, as said below
- migrant_count: int32 [256, 2], P(('slab', 'grp')), may hold values from 0 to 512
Outputs:
- saturation_out: float32 [256, 64, 256], P(('slab', 'grp'))
- size_out: float32 [1048576], P(('slab', 'grp'))
- arrivals: float32 [256, 2, 2, 512], P(('slab', 'grp'))
Inputs may be any that keep to these rules, and one draw needn't show every extreme that they name: `live_count`: about a quarter of the devices hold exactly 4096 live rows, the others a quarter to a third of that. `migrant_rows`: rows of the device's own parcels below its live count, all distinct; the list toward the lower slab lies in the lower half of the live rows, the other in the upper half.
All inputs are finite; a program needn't handle non-finite values. No bound on the sum of `inlet_mask` on one device may be relied on, other than what follows from the above.
Results may differ from a plain program's by a relative error of at most 0.00007.
Values sent between devices are 32-bit elements; how exact they have to be, the bound alone decides.
A program may use at most 64 MiB of HBM per device.

v0:
```python
import jax
import jax.numpy as jnp
from jax import lax
from jax.sharding import PartitionSpec as P

BLOCK = 2048
STEPS = 2
SUBS = 2
GROWTH = 0.08
VOLUME = 1.0
NUCLEATE = 0.02
DIFFUSE = 0.12
INLET = 4.0


def extended(cells, sides, width):
    for axis, dim in sides:
        count = lax.axis_size(axis)
        ends = count - 1
        head = lax.slice_in_dim(cells, 0, width, axis=dim)
        tail = lax.slice_in_dim(cells, cells.shape[dim] - width, cells.shape[dim], axis=dim)
        cells = jnp.concatenate(
            [
                lax.ppermute(tail, axis, [(i, (i + 1) % count) for i in range(ends)]),
                cells,
                lax.ppermute(head, axis, [((i + 1) % count, i) for i in range(ends)]),
            ],
            axis=dim,
        )
    return cells


def passed_along(value, axis, steps):
    count = lax.axis_size(axis)
    leading, last = (max(0, -steps), min(count, count - steps))
    return lax.ppermute(value, axis, [(source, source + steps) for source in range(leading, last)])


def transport(padded_x, inlet_weight):
    field_mid = padded_x[1:-1]
    padded_yz = jnp.pad(field_mid, ((0, 0), (1, 1), (1, 1)))
    beside = padded_x[2:] + padded_x[:-2]
    beside = beside + padded_yz[:, 2:, 1:-1] + padded_yz[:, :-2, 1:-1]
    beside = beside + padded_yz[:, 1:-1, 2:] + padded_yz[:, 1:-1, :-2]
    field_mid = field_mid + DIFFUSE * (beside - 6.0 * field_mid)
    return field_mid + inlet_weight * (INLET - field_mid)


def cell_tables(cells, line_count, line_width):
    line_of = cells // line_width
    place_of = cells % line_width
    hot_line = (line_of[:, None] == lax.iota(jnp.int32, line_count)[None, :]).astype(jnp.float32)
    hot_place = (place_of[:, None] == lax.iota(jnp.int32, line_width)[None, :]).astype(jnp.float32)
    return (hot_line, hot_place)


def read_cells(slab_lines, hot_line, hot_place):
    picked = jnp.dot(
        hot_line, slab_lines, precision=lax.Precision.HIGHEST, preferred_element_type=jnp.float32
    )
    return jnp.sum(picked * hot_place, axis=1)


def spread_cells(hot_line, hot_place, mass):
    return lax.dot_general(
        hot_line,
        hot_place * mass[:, None],
        (((0,), (0,)), ((), ())),
        precision=lax.Precision.HIGHEST,
        preferred_element_type=jnp.float32,
    )


def parcel_step(
    slab_lines, crystal, crystal_weight, crystal_cell, live_total, event_cell, event_count
):
    line_count, line_width = slab_lines.shape
    parcels = crystal.shape[0]
    event_line, event_place = cell_tables(event_cell, line_count, line_width)
    event_mass = (
        event_count.astype(jnp.float32)
        * NUCLEATE
        * jax.nn.softplus(read_cells(slab_lines, event_line, event_place) - 1.0)
    )
    deposit = spread_cells(event_line, event_place, event_mass)

    def one_block(block_index, state_pair):
        sizes_now, deposit_now = state_pair
        first_row = block_index * BLOCK
        part_size = lax.dynamic_slice_in_dim(sizes_now, first_row, BLOCK)
        part_weight = lax.dynamic_slice_in_dim(crystal_weight, first_row, BLOCK)
        part_cell = lax.dynamic_slice_in_dim(crystal_cell, first_row, BLOCK)
        part_live = (first_row + lax.iota(jnp.int32, BLOCK) < live_total).astype(jnp.float32)
        hot_line, hot_place = cell_tables(part_cell, line_count, line_width)
        local_sat = read_cells(slab_lines, hot_line, hot_place)
        enlarged = part_size + part_live * GROWTH * jax.nn.softplus(local_sat - 1.0)
        consumed = (
            part_live
            * part_weight
            * VOLUME
            * (enlarged * enlarged * enlarged - part_size * part_size * part_size)
        )
        sizes_now = lax.dynamic_update_slice_in_dim(sizes_now, enlarged, first_row, 0)
        return (sizes_now, deposit_now + spread_cells(hot_line, hot_place, consumed))

    block_count = parcels // BLOCK
    crystal, deposit = lax.fori_loop(0, block_count, one_block, (crystal, deposit))
    return (crystal, deposit)


def local(
    saturation,
    inlet_mask,
    crystal_size,
    crystal_weight,
    crystal_cell,
    live_count,
    nucleus_cell,
    nucleus_count,
    migrant_rows,
    migrant_count,
):
    width_z = saturation.shape[2]
    parcels = crystal_size.shape[0]
    slots = migrant_rows.shape[2]
    live_total = live_count[0]
    active_rows = (lax.iota(jnp.int32, parcels) < live_total).astype(jnp.float32)
    inlet_weight = inlet_mask.astype(jnp.float32)
    crystal = crystal_size
    field = saturation
    for step_index in range(STEPS):
        for sub_index in range(SUBS):
            substep = step_index * SUBS + sub_index
            slab_field = lax.all_gather(field, "grp", axis=0, tiled=True)
            crystal, deposit = parcel_step(
                slab_field.reshape(-1, width_z),
                crystal,
                crystal_weight,
                crystal_cell,
                live_total,
                nucleus_cell[0, substep],
                nucleus_count[0, substep],
            )
            field = field - lax.psum_scatter(
                deposit.reshape(slab_field.shape), "grp", scatter_dimension=0, tiled=True
            )
        padded_x = extended(field, ((("slab", "grp"), 0),), 1)
        field = transport(padded_x, inlet_weight)
    size_out = active_rows * crystal
    rows = migrant_rows[0]
    slot_live = (lax.iota(jnp.int32, slots)[None, :] < migrant_count[0][:, None]).astype(
        jnp.float32
    )
    sent = (
        jnp.stack([jnp.take(size_out, rows), jnp.take(crystal_weight, rows)], axis=1)
        * slot_live[:, None, :]
    )
    from_lower = passed_along(sent[1], "slab", 1)
    from_upper = passed_along(sent[0], "slab", -1)
    arrivals = jnp.stack([from_lower, from_upper], axis=0)[None]
    return (field, size_out, arrivals)


def solution(mesh):
    in_specs = (
        P(("slab", "grp"), None, None),
        P(("slab", "grp"), None, None),
        P(("slab", "grp")),
        P(("slab", "grp")),
        P(("slab", "grp")),
        P(("slab", "grp")),
        P(("slab", "grp"), None, None),
        P(("slab", "grp"), None, None),
        P(("slab", "grp"), None, None),
        P(("slab", "grp"), None),
    )
    out_specs = (
        P(("slab", "grp"), None, None),
        P(("slab", "grp")),
        P(("slab", "grp"), None, None, None),
    )
    return jax.shard_map(local, mesh=mesh, in_specs=in_specs, out_specs=out_specs, check_vma=False)
```

profile of v0, /device:TPU:24, one launch (start us, length us, event | category | flops | bytes accessed | tf_op | source)
XLA Modules:
  0.0 174.3 jit_solution(10607794521240898568)
XLA Ops:
  7.2 0.9 convert_multiply_fusion
  8.1 5.1 %all_gather.12 = f32[2,64,256]{2,1,0:T(8,128)S(1)} all-gather(f32[1,64,256]{2,1,0:T(8,128)} %param.20), channel_id=1, replica_groups=mesh['slab'=128,'grp'=2] {'grp'}, dimensions={0}, use_global_device_ids=true | all-gather | bytes 196608 | tf_op jit(solution)/shard_map/all_gather | solution.py:134
  13.3 0.5 fusion.76
  14.6 8.8 %while.68 = (s32[]{:T(128)}, f32[4096]{0:T(1024)S(1)}, f32[128,256]{1,0:T(8,128)S(1)}, s32[]{:T(128)}, s32[4096]{0:T(1024)S(1)}, /*index=5*/f32[128,256]{1,0:T(8...) while((s32[]{:T(128)}, f32[4096]{0:T(1024)S(1)}, ...), condition=%wide.region_3.4_spmd, body=%wide.region_1.3_spmd.sunk | while | flops 1614141440 | bytes 536763 | solution.py:107
  14.6 1.7 fusion.184
  16.3 0.7 fusion.185
  17.3 1.7 fusion.186
  19.1 1.7 fusion.184
  20.7 0.7 fusion.185
  21.7 1.7 fusion.186
  23.4 0.6 copy-done.9
  24.2 18.3 %reduce-scatter.5.cloned.1.call-done = f32[1,64,256]{2,1,0:T(8,128)} async-done(((f32[2,64,256]{2,1,0:T(8,128)}), f32[1,64,256]{2,1,0:T(8,128)}) %reduce-scatter.5.cloned.1.call-update) | async-done | bytes 65552 | tf_op jit(solution)/shard_map/reduce_scatter | solution.py:144
  42.5 0.8 sub.150
  43.3 4.9 %all_gather.13 = f32[2,64,256]{2,1,0:T(8,128)S(1)} all-gather(f32[1,64,256]{2,1,0:T(8,128)S(1)} %sub.150), channel_id=1, replica_groups=mesh['slab'=128,'grp'=2] {'grp'}, dimensions={0}, use_global_device_ids=true | all-gather | bytes 196608 | tf_op jit(solution)/shard_map/all_gather | solution.py:134
  48.3 0.5 fusion.77
  48.8 0.5 fusion.84
  49.3 8.8 %while.69 = (s32[]{:T(128)}, f32[4096]{0:T(1024)S(1)}, f32[128,256]{1,0:T(8,128)S(1)}, s32[]{:T(128)}, s32[4096]{0:T(1024)S(1)}, /*index=5*/f32[128,256]{1,0:T(8...) while((s32[]{:T(128)}, f32[4096]{0:T(1024)S(1)}, ...), condition=%wide.region_8.9_spmd, body=%wide.region_6.8_spmd.sunk | while | flops 1614141440 | bytes 536763 | solution.py:107
  49.4 1.7 fusion.190
  51.0 0.7 fusion.191
  52.1 1.7 fusion.192
  53.8 1.7 fusion.190
  55.5 0.7 fusion.191
  56.5 1.7 fusion.192
  58.2 0.6 copy-done.6
  59.0 16.0 %reduce-scatter.7.cloned.1.call-done = f32[1,64,256]{2,1,0:T(8,128)} async-done(((f32[2,64,256]{2,1,0:T(8,128)}), f32[1,64,256]{2,1,0:T(8,128)}) %reduce-scatter.7.cloned.1.call-update) | async-done | bytes 65552 | tf_op jit(solution)/shard_map/reduce_scatter | solution.py:144
  74.9 0.8 sub.153
  75.8 6.7 %collective-permute-start = (f32[1,64,256]{2,1,0:T(8,128)S(1)}, f32[1,64,256]{2,1,0:T(8,128)S(1)}, u32[]{:S(2)}, u32[]{:S(2)}) collective-permute-start(f32[1,64,256]{2,1,0:T(8,128)S(1)} %sub.153), channel_id=1, source_target_pairs={{1,0},{2,1},{3,2},{4,3},{5,4},{6,5},{7,6},{8,7},{9,8},{10,9},{11,1... | collective-permute-start | bytes 196616 | tf_op jit(solution)/shard_map/ppermute | solution.py:26
  82.4 1.9 %collective-permute-start.1 = (f32[1,64,256]{2,1,0:T(8,128)S(1)}, f32[1,64,256]{2,1,0:T(8,128)S(1)}, u32[]{:S(2)}, u32[]{:S(2)}) collective-permute-start(f32[1,64,256]{2,1,0:T(8,128)S(1)} %sub.153), channel_id=1, source_target_pairs={{0,1},{1,2},{2,3},{3,4},{4,5},{5,6},{6,7},{7,8},{8,9},{9,10},{10,1... | collective-permute-start | bytes 196616 | tf_op jit(solution)/shard_map/ppermute | solution.py:24
  84.4 7.8 %collective-permute-done.1 = f32[1,64,256]{2,1,0:T(8,128)S(1)} collective-permute-done((f32[1,64,256]{2,1,0:T(8,128)S(1)}, f32[1,64,256]{2,1,0:T(8,128)S(1)}, u32[]{:S(2)}, u32[]{:S(2)}) %collective-permute-start.1) | collective-permute-done | bytes 65568 | tf_op jit(solution)/shard_map/ppermute | solution.py:24
  92.3 4.9 %all_gather.14 = f32[2,64,256]{2,1,0:T(8,128)S(1)} all-gather(f32[1,64,256]{2,1,0:T(8,128)S(1)} %multiply_add_fusion.1), channel_id=1, replica_groups=mesh['slab'=128,'grp'=2] {'grp'}, dimensions={0}, use_global_device_ids=true | all-gather | bytes 196608 | tf_op jit(solution)/shard_map/all_gather | solution.py:134
  97.3 0.5 fusion.78
  97.8 0.5 fusion.82
  98.3 8.8 %while.70 = (s32[]{:T(128)}, f32[4096]{0:T(1024)S(1)}, f32[128,256]{1,0:T(8,128)S(1)}, s32[]{:T(128)}, s32[4096]{0:T(1024)S(1)}, /*index=5*/f32[128,256]{1,0:T(8...) while((s32[]{:T(128)}, f32[4096]{0:T(1024)S(1)}, ...), condition=%wide.region_13.14_spmd, body=%wide.region_11.13_spmd.sunk | while | flops 1614141440 | bytes 536763 | solution.py:107
  98.4 1.7 fusion.196
  100.1 0.7 fusion.197
  101.1 1.7 fusion.198
  102.8 1.7 fusion.196
  104.5 0.7 fusion.197
  105.5 1.7 fusion.198
  107.2 0.6 copy-done.7
  108.7 6.2 %gather_fusion.1 = f32[1024]{0:T(1024)S(1)} fusion(f32[4096]{0:T(1024)S(1)} %get-tuple-element.1170, s32[1024]{0:T(1024)S(1)} %broadcast_clamp_fusion), kind=kCustom, calls=%fused_computation.1.clone | custom fusion | bytes 12288 | tf_op jit(solution)/shard_map/jit(_take)/gather | solution.py:155
  114.8 2.1 %reduce-scatter.9.cloned.1.call-done = f32[1,64,256]{2,1,0:T(8,128)} async-done(((f32[2,64,256]{2,1,0:T(8,128)}), f32[1,64,256]{2,1,0:T(8,128)}) %reduce-scatter.9.cloned.1.call-update) | async-done | bytes 65552 | tf_op jit(solution)/shard_map/reduce_scatter | solution.py:144
  117.0 0.8 sub.158
  117.8 5.1 %all_gather.15 = f32[2,64,256]{2,1,0:T(8,128)S(1)} all-gather(f32[1,64,256]{2,1,0:T(8,128)S(1)} %sub.158), channel_id=1, replica_groups=mesh['slab'=128,'grp'=2] {'grp'}, dimensions={0}, use_global_device_ids=true | all-gather | bytes 196608 | tf_op jit(solution)/shard_map/all_gather | solution.py:134
  123.0 0.5 fusion.79
  123.5 0.5 fusion.80
  124.0 8.8 %while.71 = (s32[]{:T(128)}, f32[4096]{0:T(1024)S(1)}, f32[128,256]{1,0:T(8,128)S(1)}, s32[]{:T(128)}, s32[4096]{0:T(1024)S(1)}, /*index=5*/f32[128,256]{1,0:T(8...) while((s32[]{:T(128)}, f32[4096]{0:T(1024)S(1)}, ...), condition=%wide.region_18.19_spmd, body=%wide.region_16.18_spmd.sunk | while | flops 1614141440 | bytes 536763 | solution.py:107
  124.1 1.7 fusion.202
  125.7 0.7 fusion.203
  126.7 1.7 fusion.204
  128.5 1.7 fusion.202
  130.2 0.7 fusion.203
  131.1 1.7 fusion.204
  132.9 0.6 copy-done.8
  133.6 6.2 %gather_fusion = f32[1024]{0:T(1024)S(1)} fusion(f32[4096]{0:T(1024)S(1)} %fusion.130, s32[1024]{0:T(1024)S(1)} %broadcast_clamp_fusion), kind=kCustom, calls=%fused_computation.clone | custom fusion | bytes 12288 | tf_op jit(solution)/shard_map/jit(_take)/gather | solution.py:155
  139.8 5.6 %collective-permute-start.5 = (f32[2,512]{1,0:T(2,128)S(1)}, f32[2,512]{1,0:T(2,128)S(1)}, u32[]{:S(2)}, u32[]{:S(2)}) collective-permute-start(f32[2,512]{1,0:T(2,128)S(1)} %get-tuple-element.809), channel_id=1, source_target_pairs={{2,0},{4,2},{6,4},{8,6},{10,8},{12,10},{14,12},{16,14},{18,16},{20... | collective-permute-start | bytes 12296 | tf_op jit(solution)/shard_map/ppermute | solution.py:36
  145.4 1.9 %collective-permute-start.4 = (f32[2,512]{1,0:T(2,128)S(1)}, f32[2,512]{1,0:T(2,128)S(1)}, u32[]{:S(2)}, u32[]{:S(2)}) collective-permute-start(f32[2,512]{1,0:T(2,128)S(1)} %get-tuple-element.808), channel_id=1, source_target_pairs={{0,2},{2,4},{4,6},{6,8},{8,10},{10,12},{12,14},{14,16},{16,18},{18... | collective-permute-start | bytes 12296 | tf_op jit(solution)/shard_map/ppermute | solution.py:36
  147.3 2.3 %reduce-scatter.11.cloned.1.call-done = f32[1,64,256]{2,1,0:T(8,128)} async-done(((f32[2,64,256]{2,1,0:T(8,128)}), f32[1,64,256]{2,1,0:T(8,128)}) %reduce-scatter.11.cloned.1.call-update) | async-done | bytes 65552 | tf_op jit(solution)/shard_map/reduce_scatter | solution.py:144
  149.6 0.8 sub.161
  150.5 6.7 %collective-permute-start.2 = (f32[1,64,256]{2,1,0:T(8,128)S(1)}, f32[1,64,256]{2,1,0:T(8,128)S(1)}, u32[]{:S(2)}, u32[]{:S(2)}) collective-permute-start(f32[1,64,256]{2,1,0:T(8,128)S(1)} %sub.161), channel_id=1, source_target_pairs={{1,0},{2,1},{3,2},{4,3},{5,4},{6,5},{7,6},{8,7},{9,8},{10,9},{11,1... | collective-permute-start | bytes 196616 | tf_op jit(solution)/shard_map/ppermute | solution.py:26
  157.2 1.9 %collective-permute-start.3 = (f32[1,64,256]{2,1,0:T(8,128)S(1)}, f32[1,64,256]{2,1,0:T(8,128)S(1)}, u32[]{:S(2)}, u32[]{:S(2)}) collective-permute-start(f32[1,64,256]{2,1,0:T(8,128)S(1)} %sub.161), channel_id=1, source_target_pairs={{0,1},{1,2},{2,3},{3,4},{4,5},{5,6},{6,7},{7,8},{8,9},{9,10},{10,1... | collective-permute-start | bytes 196616 | tf_op jit(solution)/shard_map/ppermute | solution.py:24
  159.1 0.6 maximum_bitcast_fusion
  159.7 7.2 %collective-permute-done.3 = f32[1,64,256]{2,1,0:T(8,128)S(1)} collective-permute-done((f32[1,64,256]{2,1,0:T(8,128)S(1)}, f32[1,64,256]{2,1,0:T(8,128)S(1)}, u32[]{:S(2)}, u32[]{:S(2)}) %collective-permute-start.3) | collective-permute-done | bytes 65568 | tf_op jit(solution)/shard_map/ppermute | solution.py:24
  167.0 0.7 multiply_add_fusion
  (81 shorter events, 4.1 us)
Async XLA Ops:
  7.2 6.1 %copy-start.11 = (s32[1,4,512]{2,1,0:T(4,128)S(1)}, s32[1,4,512]{2,1,0:T(4,128)}, u32[]{:S(2)}) copy-start(s32[1,4,512]{2,1,0:T(4,128)} %param.26) | copy-start | bytes 24580
  7.2 35.3 %reduce-scatter.5.cloned.1.call-start = ((), (), s32[]{:S(2)}) async-start(), calls=%async_computation.4 | async-start | bytes 196608 | tf_op jit(solution)/shard_map/reduce_scatter | solution.py:144
  13.8 0.7 copy-start
  13.8 0.7 copy-start.2
  13.8 0.7 copy-start.3
  23.4 0.7 copy-start.9
  23.4 19.1 %copy-start.4 = (f32[1,64,256]{2,1,0:T(8,128)S(1)}, f32[1,64,256]{2,1,0:T(8,128)}, u32[]{:S(2)}) copy-start(f32[1,64,256]{2,1,0:T(8,128)} %param.20) | copy-start | bytes 196612
  24.1 50.8 %reduce-scatter.7.cloned.1.call-start = ((), (), s32[]{:S(2)}) async-start(), calls=%async_computation.5 | async-start | bytes 196608 | tf_op jit(solution)/shard_map/reduce_scatter | solution.py:144
  58.2 0.7 copy-start.6
  58.2 0.7 copy-start.10
  58.9 33.4 %copy-start.5 = (s32[1,64,256]{2,1,0:T(8,128)S(1)}, s32[1,64,256]{2,1,0:T(8,128)}, u32[]{:S(2)}) copy-start(s32[1,64,256]{2,1,0:T(8,128)} %param.21) | copy-start | bytes 196612
  58.9 58.1 %reduce-scatter.9.cloned.1.call-start = ((), (), s32[]{:S(2)}) async-start(), calls=%async_computation.6 | async-start | bytes 196608 | tf_op jit(solution)/shard_map/reduce_scatter | solution.py:144
  75.8 8.6 %collective-permute-start = (f32[1,64,256]{2,1,0:T(8,128)S(1)}, f32[1,64,256]{2,1,0:T(8,128)S(1)}, u32[]{:S(2)}, u32[]{:S(2)}) collective-permute-start(f32[1,64,256]{2,1,0:T(8,128)S(1)} %sub.153), channel_id=1, source_target_pairs={{1,0},{2,1},{3,2},{4,3},{5,4},{6,5},{7,6},{8,7},{9,8},{10,9},{11,1... | collective-permute-start | bytes 196616 | tf_op jit(solution)/shard_map/ppermute | solution.py:26
  82.4 9.8 %collective-permute-start.1 = (f32[1,64,256]{2,1,0:T(8,128)S(1)}, f32[1,64,256]{2,1,0:T(8,128)S(1)}, u32[]{:S(2)}, u32[]{:S(2)}) collective-permute-start(f32[1,64,256]{2,1,0:T(8,128)S(1)} %sub.153), channel_id=1, source_target_pairs={{0,1},{1,2},{2,3},{3,4},{4,5},{5,6},{6,7},{7,8},{8,9},{9,10},{10,1... | collective-permute-start | bytes 196616 | tf_op jit(solution)/shard_map/ppermute | solution.py:24
  107.2 0.7 copy-start.7
  107.2 0.7 copy-start.12
  107.9 41.8 %reduce-scatter.11.cloned.1.call-start = ((), (), s32[]{:S(2)}) async-start(), calls=%async_computation.7 | async-start | bytes 196608 | tf_op jit(solution)/shard_map/reduce_scatter | solution.py:144
  132.9 0.7 copy-start.8
  133.6 6.2 %copy-start.1 = (f32[4096]{0:T(1024)}, f32[4096]{0:T(1024)S(1)}, u32[]{:S(2)}) copy-start(f32[4096]{0:T(1024)S(1)} %fusion.130) | copy-start | bytes 49156
  139.8 19.3 %collective-permute-start.5 = (f32[2,512]{1,0:T(2,128)S(1)}, f32[2,512]{1,0:T(2,128)S(1)}, u32[]{:S(2)}, u32[]{:S(2)}) collective-permute-start(f32[2,512]{1,0:T(2,128)S(1)} %get-tuple-element.809), channel_id=1, source_target_pairs={{2,0},{4,2},{6,4},{8,6},{10,8},{12,10},{14,12},{16,14},{18,16},{20... | collective-permute-start | bytes 12296 | tf_op jit(solution)/shard_map/ppermute | solution.py:36
  145.4 13.7 %collective-permute-start.4 = (f32[2,512]{1,0:T(2,128)S(1)}, f32[2,512]{1,0:T(2,128)S(1)}, u32[]{:S(2)}, u32[]{:S(2)}) collective-permute-start(f32[2,512]{1,0:T(2,128)S(1)} %get-tuple-element.808), channel_id=1, source_target_pairs={{0,2},{2,4},{4,6},{6,8},{8,10},{10,12},{12,14},{14,16},{16,18},{18... | collective-permute-start | bytes 12296 | tf_op jit(solution)/shard_map/ppermute | solution.py:36
  150.5 9.3 %collective-permute-start.2 = (f32[1,64,256]{2,1,0:T(8,128)S(1)}, f32[1,64,256]{2,1,0:T(8,128)S(1)}, u32[]{:S(2)}, u32[]{:S(2)}) collective-permute-start(f32[1,64,256]{2,1,0:T(8,128)S(1)} %sub.161), channel_id=1, source_target_pairs={{1,0},{2,1},{3,2},{4,3},{5,4},{6,5},{7,6},{8,7},{9,8},{10,9},{11,1... | collective-permute-start | bytes 196616 | tf_op jit(solution)/shard_map/ppermute | solution.py:26
  157.2 9.8 %collective-permute-start.3 = (f32[1,64,256]{2,1,0:T(8,128)S(1)}, f32[1,64,256]{2,1,0:T(8,128)S(1)}, u32[]{:S(2)}, u32[]{:S(2)}) collective-permute-start(f32[1,64,256]{2,1,0:T(8,128)S(1)} %sub.161), channel_id=1, source_target_pairs={{0,1},{1,2},{2,3},{3,4},{4,5},{5,6},{6,7},{7,8},{8,9},{9,10},{10,1... | collective-permute-start | bytes 196616 | tf_op jit(solution)/shard_map/ppermute | solution.py:24
Sparse Core Ops, SparseCore 0:
  24.2 18.2 reduce-scatter.4
  59.0 15.8 reduce-scatter.6
  108.0 8.9 reduce-scatter.8
  133.7 15.9 reduce-scatter.10
where the time goes:
time: 175 us; the launch traced here: 174 us
  waiting for transfers between devices  53.9 us (31%)
  matrix products  30.9 us (18%)
  starting transfers between devices  24.9 us (14%)
  blocking collectives  20.1 us (11%)
  local copies, waits for them, and re-layouts  17.7 us (10%)
  between operations  14.9 us (9%)
  other arithmetic  11.5 us (7%)
    reduce_scatter x4, waiting for transfers between devices, local(): lax.psum_scatter(deposit.reshape(slab_field.shape), 'grp', scatter_dimens...  38.7 us
    all_gather x4, blocking collectives, local(): slab_field = lax.all_gather(field, 'grp', axis=0, tiled=True)  20.1 us
    dot_general x12, matrix products, spread_cells(): lax.dot_general(hot_line, hot_place * mass[:, None], (((0,), (0,)), ((),...  15.5 us
    dot_general x12, matrix products, read_cells(): jnp.dot(hot_line, slab_lines, precision=lax.Precision.HIGHEST, preferred_...  15.4 us
    ppermute x2, waiting for transfers between devices, extended(): lax.ppermute(tail, axis, [(i, (i + 1) % count) for i in range(ends)])  15.1 us
    ppermute x2, starting transfers between devices, extended(): lax.ppermute(head, axis, [((i + 1) % count, i) for i in range(ends)])  13.3 us
    ppermute x2, starting transfers between devices, passed_along(): lax.ppermute(value, axis, [(source, source + steps) for source in range(l...  7.5 us
    gather x2, local copies, waits for them, and re-layouts, local(): jnp.take(crystal_weight, rows)  6.16 us
  transfers between devices with their start and end apart: 10, of which 6 were waited for; matrix products, arithmetic and copies ran while one was open for 8% of the time, Pallas kernels for 0%

commit v1 on v0

--- a/solution.py
+++ b/solution.py
@@ -2,6 +2,7 @@
 import jax.numpy as jnp
 from jax import lax
 from jax.sharding import PartitionSpec as P
+from jax.lax import all_to_all, axis_size
 
 BLOCK = 2048
 STEPS = 2
@@ -11,6 +12,10 @@
 NUCLEATE = 0.02
 DIFFUSE = 0.12
 INLET = 4.0
+
+
+def apply_the_files(base_x, across):
+    return jnp.concatenate(all_to_all(jnp.stack(axis_size(across) * [base_x], 0), across, 0, 0), 0)
 
 
 def extended(cells, sides, width):
@@ -131,7 +136,7 @@
     for step_index in range(STEPS):
         for sub_index in range(SUBS):
             substep = step_index * SUBS + sub_index
-            slab_field = lax.all_gather(field, "grp", axis=0, tiled=True)
+            slab_field = apply_the_files(field, "grp")
             crystal, deposit = parcel_step(
                 slab_field.reshape(-1, width_z),
                 crystal,

time: 175 us -> 189 us (1.080)
  blocking collectives: 20.1 us -> 0 us
  waiting for transfers between devices: 53.9 us -> 71.4 us
  starting transfers between devices: 24.9 us -> 38.7 us
  other arithmetic: 11.5 us -> 14.2 us
    all_gather x4 -> x0, blocking collectives: 20.1 us -> none  [local(): slab_field = lax.all_gather(field, 'grp', axis=0, tiled=True)]
    all_to_all x0 -> x4, waiting for transfers between devices: none -> 17.3 us  [apply_the_files(): all_to_all(jnp.stack(axis_size(across) * [base_x], 0), across, 0, 0)]
    all_to_all x0 -> x4, starting transfers between devices: none -> 13.8 us  [apply_the_files(): all_to_all(jnp.stack(axis_size(across) * [base_x], 0), across, 0, 0)]
    another operation x0 -> x4, other arithmetic: none -> 3.52 us  [apply_the_files(): jnp.stack(axis_size(across) * [base_x], 0)]
  transfers between devices with their start and end apart: 10 -> 14, of which waited for: 6 -> 10; matrix products, arithmetic and copies ran while one was open for 8% -> 7% of each run, Pallas kernels for 0% -> 0%
where the time goes in v1:
time: 189 us; the launch traced here: 188 us
  waiting for transfers between devices  71.4 us (38%)
  starting transfers between devices  38.7 us (20%)
  matrix products  30.9 us (16%)
  local copies, waits for them, and re-layouts  17.6 us (9%)
  between operations  14.9 us (8%)
  other arithmetic  14.2 us (8%)
    reduce_scatter x4, waiting for transfers between devices, local(): lax.psum_scatter(deposit.reshape(slab_field.shape), 'grp', scatter_dimens...  39 us
    all_to_all x4, waiting for transfers between devices, apply_the_files(): all_to_all(jnp.stack(axis_size(across) * [base_x], 0), across, 0, 0)  17.3 us
    dot_general x12, matrix products, spread_cells(): lax.dot_general(hot_line, hot_place * mass[:, None], (((0,), (0,)), ((),...  15.5 us
    dot_general x12, matrix products, read_cells(): jnp.dot(hot_line, slab_lines, precision=lax.Precision.HIGHEST, preferred_...  15.4 us
    ppermute x2, waiting for transfers between devices, extended(): lax.ppermute(tail, axis, [(i, (i + 1) % count) for i in range(ends)])  15.1 us
    all_to_all x4, starting transfers between devices, apply_the_files(): all_to_all(jnp.stack(axis_size(across) * [base_x], 0), across, 0, 0)  13.8 us
    ppermute x2, starting transfers between devices, extended(): lax.ppermute(head, axis, [((i + 1) % count, i) for i in range(ends)])  13.3 us
    ppermute x2, starting transfers between devices, passed_along(): lax.ppermute(value, axis, [(source, source + steps) for source in range(l...  7.5 us
  transfers between devices with their start and end apart: 14, of which 10 were waited for; matrix products, arithmetic and copies ran while one was open for 7% of the time, Pallas kernels for 0%

profile of v1, /device:TPU:24, one launch (start us, length us, event | category | flops | bytes accessed | tf_op | source)
XLA Modules:
  0.0 188.2 jit_solution(1140903395453480010)
XLA Ops:
  7.2 1.6 pad_maximum_fusion
  8.7 3.5 %all-to-all-start = ((f32[2,1,64,256]{3,2,1,0:T(8,128)}), f32[2,1,64,256]{3,2,1,0:T(8,128)S(1)}, u32[]{:S(2)}, u32[]{:S(2)}) async-start(f32[2,1,64,256]{3,2,1,0:T(8,128)} %pad_maximum_fusion), calls=%async_computation | async-start | bytes 262144 | tf_op jit(solution)/shard_map/all_to_all | solution.py:18
  12.4 4.3 %all-to-all-done = f32[2,1,64,256]{3,2,1,0:T(8,128)S(1)} async-done(((f32[2,1,64,256]{3,2,1,0:T(8,128)}), f32[2,1,64,256]{3,2,1,0:T(8,128)S(1)}, u32[]{:S(2)}, u32[]{:S(2)}) %all-to-all-start) | async-done | bytes 131104 | tf_op jit(solution)/shard_map/all_to_all | solution.py:18
  18.0 8.8 %while.68 = (s32[]{:T(128)}, f32[4096]{0:T(1024)S(1)}, f32[128,256]{1,0:T(8,128)S(1)}, s32[]{:T(128)}, s32[4096]{0:T(1024)S(1)}, /*index=5*/f32[128,256]{1,0:T(8...) while((s32[]{:T(128)}, f32[4096]{0:T(1024)S(1)}, ...), condition=%wide.region_3.4_spmd, body=%wide.region_1.3_spmd.sunk | while | flops 1614141440 | bytes 536763 | solution.py:112
  18.1 1.7 fusion.184
  19.7 0.7 fusion.185
  20.7 1.7 fusion.186
  22.5 1.7 fusion.184
  24.2 0.7 fusion.185
  25.1 1.7 fusion.186
  26.9 0.6 copy-done.9
  27.5 18.4 %reduce-scatter.5.cloned.1.call-done = f32[1,64,256]{2,1,0:T(8,128)} async-done(((f32[2,64,256]{2,1,0:T(8,128)}), f32[1,64,256]{2,1,0:T(8,128)}) %reduce-scatter.5.cloned.1.call-update) | async-done | bytes 65552 | tf_op jit(solution)/shard_map/reduce_scatter | solution.py:149
  45.9 0.8 sub.150
  46.8 0.7 pad_maximum_fusion.1
  47.4 3.4 %all-to-all-start.1 = ((f32[2,1,64,256]{3,2,1,0:T(8,128)}), f32[2,1,64,256]{3,2,1,0:T(8,128)S(1)}, u32[]{:S(2)}, u32[]{:S(2)}) async-start(f32[2,1,64,256]{3,2,1,0:T(8,128)} %pad_maximum_fusion.1), calls=%async_computation.2 | async-start | bytes 262144 | tf_op jit(solution)/shard_map/all_to_all | solution.py:18
  50.9 4.4 %all-to-all-done.1 = f32[2,1,64,256]{3,2,1,0:T(8,128)S(1)} async-done(((f32[2,1,64,256]{3,2,1,0:T(8,128)}), f32[2,1,64,256]{3,2,1,0:T(8,128)S(1)}, u32[]{:S(2)}, u32[]{:S(2)}) %all-to-all-start.1) | async-done | bytes 131104 | tf_op jit(solution)/shard_map/all_to_all | solution.py:18
  56.3 8.8 %while.69 = (s32[]{:T(128)}, f32[4096]{0:T(1024)S(1)}, f32[128,256]{1,0:T(8,128)S(1)}, s32[]{:T(128)}, s32[4096]{0:T(1024)S(1)}, /*index=5*/f32[128,256]{1,0:T(8...) while((s32[]{:T(128)}, f32[4096]{0:T(1024)S(1)}, ...), condition=%wide.region_8.9_spmd, body=%wide.region_6.8_spmd.sunk | while | flops 1614141440 | bytes 536763 | solution.py:112
  56.4 1.7 fusion.190
  58.0 0.7 fusion.191
  59.0 1.7 fusion.192
  60.8 1.7 fusion.190
  62.5 0.7 fusion.191
  63.4 1.7 fusion.192
  65.2 0.6 copy-done.6
  65.8 16.0 %reduce-scatter.7.cloned.1.call-done = f32[1,64,256]{2,1,0:T(8,128)} async-done(((f32[2,64,256]{2,1,0:T(8,128)}), f32[1,64,256]{2,1,0:T(8,128)}) %reduce-scatter.7.cloned.1.call-update) | async-done | bytes 65552 | tf_op jit(solution)/shard_map/reduce_scatter | solution.py:149
  81.9 0.8 sub.153
  82.7 6.6 %collective-permute-start = (f32[1,64,256]{2,1,0:T(8,128)S(1)}, f32[1,64,256]{2,1,0:T(8,128)S(1)}, u32[]{:S(2)}, u32[]{:S(2)}) collective-permute-start(f32[1,64,256]{2,1,0:T(8,128)S(1)} %sub.153), channel_id=1, source_target_pairs={{1,0},{2,1},{3,2},{4,3},{5,4},{6,5},{7,6},{8,7},{9,8},{10,9},{11,1... | collective-permute-start | bytes 196616 | tf_op jit(solution)/shard_map/ppermute | solution.py:31
  89.4 1.9 %collective-permute-start.1 = (f32[1,64,256]{2,1,0:T(8,128)S(1)}, f32[1,64,256]{2,1,0:T(8,128)S(1)}, u32[]{:S(2)}, u32[]{:S(2)}) collective-permute-start(f32[1,64,256]{2,1,0:T(8,128)S(1)} %sub.153), channel_id=1, source_target_pairs={{0,1},{1,2},{2,3},{3,4},{4,5},{5,6},{6,7},{7,8},{8,9},{9,10},{10,1... | collective-permute-start | bytes 196616 | tf_op jit(solution)/shard_map/ppermute | solution.py:29
  91.4 7.8 %collective-permute-done.1 = f32[1,64,256]{2,1,0:T(8,128)S(1)} collective-permute-done((f32[1,64,256]{2,1,0:T(8,128)S(1)}, f32[1,64,256]{2,1,0:T(8,128)S(1)}, u32[]{:S(2)}, u32[]{:S(2)}) %collective-permute-start.1) | collective-permute-done | bytes 65568 | tf_op jit(solution)/shard_map/ppermute | solution.py:29
  99.3 0.7 pad_maximum_fusion.2
  100.0 3.4 %all-to-all-start.2 = ((f32[2,1,64,256]{3,2,1,0:T(8,128)}), f32[2,1,64,256]{3,2,1,0:T(8,128)S(1)}, u32[]{:S(2)}, u32[]{:S(2)}) async-start(f32[2,1,64,256]{3,2,1,0:T(8,128)} %pad_maximum_fusion.2), calls=%async_computation.4 | async-start | bytes 262144 | tf_op jit(solution)/shard_map/all_to_all | solution.py:18
  103.4 4.4 %all-to-all-done.2 = f32[2,1,64,256]{3,2,1,0:T(8,128)S(1)} async-done(((f32[2,1,64,256]{3,2,1,0:T(8,128)}), f32[2,1,64,256]{3,2,1,0:T(8,128)S(1)}, u32[]{:S(2)}, u32[]{:S(2)}) %all-to-all-start.2) | async-done | bytes 131104 | tf_op jit(solution)/shard_map/all_to_all | solution.py:18
  108.8 8.8 %while.70 = (s32[]{:T(128)}, f32[4096]{0:T(1024)S(1)}, f32[128,256]{1,0:T(8,128)S(1)}, s32[]{:T(128)}, s32[4096]{0:T(1024)S(1)}, /*index=5*/f32[128,256]{1,0:T(8...) while((s32[]{:T(128)}, f32[4096]{0:T(1024)S(1)}, ...), condition=%wide.region_13.14_spmd, body=%wide.region_11.13_spmd.sunk | while | flops 1614141440 | bytes 536763 | solution.py:112
  108.9 1.7 fusion.196
  110.6 0.7 fusion.197
  111.6 1.7 fusion.198
  113.4 1.7 fusion.196
  115.0 0.7 fusion.197
  116.0 1.7 fusion.198
  117.7 0.6 copy-done.7
  119.0 6.2 %gather_fusion.1 = f32[1024]{0:T(1024)S(1)} fusion(f32[4096]{0:T(1024)S(1)} %get-tuple-element.1170, s32[1024]{0:T(1024)S(1)} %broadcast_clamp_fusion), kind=kCustom, calls=%fused_computation.1.clone | custom fusion | bytes 12288 | tf_op jit(solution)/shard_map/jit(_take)/gather | solution.py:160
  125.2 2.3 %reduce-scatter.9.cloned.1.call-done = f32[1,64,256]{2,1,0:T(8,128)} async-done(((f32[2,64,256]{2,1,0:T(8,128)}), f32[1,64,256]{2,1,0:T(8,128)}) %reduce-scatter.9.cloned.1.call-update) | async-done | bytes 65552 | tf_op jit(solution)/shard_map/reduce_scatter | solution.py:149
  127.5 0.8 sub.158
  128.3 0.7 pad_maximum_fusion.3
  129.0 3.5 %all-to-all-start.3 = ((f32[2,1,64,256]{3,2,1,0:T(8,128)}), f32[2,1,64,256]{3,2,1,0:T(8,128)S(1)}, u32[]{:S(2)}, u32[]{:S(2)}) async-start(f32[2,1,64,256]{3,2,1,0:T(8,128)} %pad_maximum_fusion.3), calls=%async_computation.6 | async-start | bytes 262144 | tf_op jit(solution)/shard_map/all_to_all | solution.py:18
  132.8 4.1 %all-to-all-done.3 = f32[2,1,64,256]{3,2,1,0:T(8,128)S(1)} async-done(((f32[2,1,64,256]{3,2,1,0:T(8,128)}), f32[2,1,64,256]{3,2,1,0:T(8,128)S(1)}, u32[]{:S(2)}, u32[]{:S(2)}) %all-to-all-start.3) | async-done | bytes 131104 | tf_op jit(solution)/shard_map/all_to_all | solution.py:18
  138.0 8.8 %while.71 = (s32[]{:T(128)}, f32[4096]{0:T(1024)S(1)}, f32[128,256]{1,0:T(8,128)S(1)}, s32[]{:T(128)}, s32[4096]{0:T(1024)S(1)}, /*index=5*/f32[128,256]{1,0:T(8...) while((s32[]{:T(128)}, f32[4096]{0:T(1024)S(1)}, ...), condition=%wide.region_18.19_spmd, body=%wide.region_16.18_spmd.sunk | while | flops 1614141440 | bytes 536763 | solution.py:112
  138.1 1.7 fusion.202
  139.7 0.7 fusion.203
  140.7 1.7 fusion.204
  142.5 1.7 fusion.202
  144.2 0.7 fusion.203
  145.2 1.7 fusion.204
  146.9 0.6 copy-done.8
  147.6 6.2 %gather_fusion = f32[1024]{0:T(1024)S(1)} fusion(f32[4096]{0:T(1024)S(1)} %fusion.130, s32[1024]{0:T(1024)S(1)} %broadcast_clamp_fusion), kind=kCustom, calls=%fused_computation.clone | custom fusion | bytes 12288 | tf_op jit(solution)/shard_map/jit(_take)/gather | solution.py:160
  153.8 5.6 %collective-permute-start.5 = (f32[2,512]{1,0:T(2,128)S(1)}, f32[2,512]{1,0:T(2,128)S(1)}, u32[]{:S(2)}, u32[]{:S(2)}) collective-permute-start(f32[2,512]{1,0:T(2,128)S(1)} %get-tuple-element.809), channel_id=1, source_target_pairs={{2,0},{4,2},{6,4},{8,6},{10,8},{12,10},{14,12},{16,14},{18,16},{20... | collective-permute-start | bytes 12296 | tf_op jit(solution)/shard_map/ppermute | solution.py:41
  159.4 1.9 %collective-permute-start.4 = (f32[2,512]{1,0:T(2,128)S(1)}, f32[2,512]{1,0:T(2,128)S(1)}, u32[]{:S(2)}, u32[]{:S(2)}) collective-permute-start(f32[2,512]{1,0:T(2,128)S(1)} %get-tuple-element.808), channel_id=1, source_target_pairs={{0,2},{2,4},{4,6},{6,8},{8,10},{10,12},{12,14},{14,16},{16,18},{18... | collective-permute-start | bytes 12296 | tf_op jit(solution)/shard_map/ppermute | solution.py:41
  161.3 2.3 %reduce-scatter.11.cloned.1.call-done = f32[1,64,256]{2,1,0:T(8,128)} async-done(((f32[2,64,256]{2,1,0:T(8,128)}), f32[1,64,256]{2,1,0:T(8,128)}) %reduce-scatter.11.cloned.1.call-update) | async-done | bytes 65552 | tf_op jit(solution)/shard_map/reduce_scatter | solution.py:149
  163.6 0.8 sub.161
  164.5 6.6 %collective-permute-start.2 = (f32[1,64,256]{2,1,0:T(8,128)S(1)}, f32[1,64,256]{2,1,0:T(8,128)S(1)}, u32[]{:S(2)}, u32[]{:S(2)}) collective-permute-start(f32[1,64,256]{2,1,0:T(8,128)S(1)} %sub.161), channel_id=1, source_target_pairs={{1,0},{2,1},{3,2},{4,3},{5,4},{6,5},{7,6},{8,7},{9,8},{10,9},{11,1... | collective-permute-start | bytes 196616 | tf_op jit(solution)/shard_map/ppermute | solution.py:31
  171.1 1.9 %collective-permute-start.3 = (f32[1,64,256]{2,1,0:T(8,128)S(1)}, f32[1,64,256]{2,1,0:T(8,128)S(1)}, u32[]{:S(2)}, u32[]{:S(2)}) collective-permute-start(f32[1,64,256]{2,1,0:T(8,128)S(1)} %sub.161), channel_id=1, source_target_pairs={{0,1},{1,2},{2,3},{3,4},{4,5},{5,6},{6,7},{7,8},{8,9},{9,10},{10,1... | collective-permute-start | bytes 196616 | tf_op jit(solution)/shard_map/ppermute | solution.py:29
  173.1 0.6 maximum_bitcast_fusion
  173.7 7.2 %collective-permute-done.3 = f32[1,64,256]{2,1,0:T(8,128)S(1)} collective-permute-done((f32[1,64,256]{2,1,0:T(8,128)S(1)}, f32[1,64,256]{2,1,0:T(8,128)S(1)}, u32[]{:S(2)}, u32[]{:S(2)}) %collective-permute-start.3) | collective-permute-done | bytes 65568 | tf_op jit(solution)/shard_map/ppermute | solution.py:29
  180.9 0.7 multiply_add_fusion
  (91 shorter events, 7.9 us)
Async XLA Ops:
  8.7 3.6 %copy-start.11 = (s32[1,4,512]{2,1,0:T(4,128)S(1)}, s32[1,4,512]{2,1,0:T(4,128)}, u32[]{:S(2)}) copy-start(s32[1,4,512]{2,1,0:T(4,128)} %param.27) | copy-start | bytes 24580
  8.7 3.6 %copy-start.12 = (s32[1,4,512]{2,1,0:T(4,128)S(1)}, s32[1,4,512]{2,1,0:T(4,128)}, u32[]{:S(2)}) copy-start(s32[1,4,512]{2,1,0:T(4,128)} %param.26) | copy-start | bytes 24580
  8.7 8.0 %all-to-all-start = ((f32[2,1,64,256]{3,2,1,0:T(8,128)}), f32[2,1,64,256]{3,2,1,0:T(8,128)S(1)}, u32[]{:S(2)}, u32[]{:S(2)}) async-start(f32[2,1,64,256]{3,2,1,0:T(8,128)} %pad_maximum_fusion), calls=%async_computation | async-start | bytes 262144 | tf_op jit(solution)/shard_map/all_to_all | solution.py:18
  12.2 33.7 %reduce-scatter.5.cloned.1.call-start = ((), (), s32[]{:S(2)}) async-start(), calls=%async_computation.8 | async-start | bytes 196608 | tf_op jit(solution)/shard_map/reduce_scatter | solution.py:149
  17.3 0.7 copy-start
  17.3 0.7 copy-start.2
  17.3 0.7 copy-start.3
  26.8 0.6 copy-start.9
  26.9 19.0 %copy-start.4 = (f32[1,64,256]{2,1,0:T(8,128)S(1)}, f32[1,64,256]{2,1,0:T(8,128)}, u32[]{:S(2)}) copy-start(f32[1,64,256]{2,1,0:T(8,128)} %param.20) | copy-start | bytes 196612
  47.4 7.8 %all-to-all-start.1 = ((f32[2,1,64,256]{3,2,1,0:T(8,128)}), f32[2,1,64,256]{3,2,1,0:T(8,128)S(1)}, u32[]{:S(2)}, u32[]{:S(2)}) async-start(f32[2,1,64,256]{3,2,1,0:T(8,128)} %pad_maximum_fusion.1), calls=%async_computation.2 | async-start | bytes 262144 | tf_op jit(solution)/shard_map/all_to_all | solution.py:18
  50.8 31.1 %reduce-scatter.7.cloned.1.call-start = ((), (), s32[]{:S(2)}) async-start(), calls=%async_computation.9 | async-start | bytes 196608 | tf_op jit(solution)/shard_map/reduce_scatter | solution.py:149
  65.1 0.6 copy-start.6
  65.8 25.5 %copy-start.10 = (s32[1,2,512]{2,1,0:T(2,128)S(1)}, s32[1,2,512]{2,1,0:T(2,128)}, u32[]{:S(2)}) copy-start(s32[1,2,512]{2,1,0:T(2,128)} %param.28) | copy-start | bytes 12292
  65.8 33.4 %copy-start.5 = (s32[1,64,256]{2,1,0:T(8,128)S(1)}, s32[1,64,256]{2,1,0:T(8,128)}, u32[]{:S(2)}) copy-start(s32[1,64,256]{2,1,0:T(8,128)} %param.21) | copy-start | bytes 196612
  82.7 8.6 %collective-permute-start = (f32[1,64,256]{2,1,0:T(8,128)S(1)}, f32[1,64,256]{2,1,0:T(8,128)S(1)}, u32[]{:S(2)}, u32[]{:S(2)}) collective-permute-start(f32[1,64,256]{2,1,0:T(8,128)S(1)} %sub.153), channel_id=1, source_target_pairs={{1,0},{2,1},{3,2},{4,3},{5,4},{6,5},{7,6},{8,7},{9,8},{10,9},{11,1... | collective-permute-start | bytes 196616 | tf_op jit(solution)/shard_map/ppermute | solution.py:31
  89.4 9.8 %collective-permute-start.1 = (f32[1,64,256]{2,1,0:T(8,128)S(1)}, f32[1,64,256]{2,1,0:T(8,128)S(1)}, u32[]{:S(2)}, u32[]{:S(2)}) collective-permute-start(f32[1,64,256]{2,1,0:T(8,128)S(1)} %sub.153), channel_id=1, source_target_pairs={{0,1},{1,2},{2,3},{3,4},{4,5},{5,6},{6,7},{7,8},{8,9},{9,10},{10,1... | collective-permute-start | bytes 196616 | tf_op jit(solution)/shard_map/ppermute | solution.py:29
  100.0 7.8 %all-to-all-start.2 = ((f32[2,1,64,256]{3,2,1,0:T(8,128)}), f32[2,1,64,256]{3,2,1,0:T(8,128)S(1)}, u32[]{:S(2)}, u32[]{:S(2)}) async-start(f32[2,1,64,256]{3,2,1,0:T(8,128)} %pad_maximum_fusion.2), calls=%async_computation.4 | async-start | bytes 262144 | tf_op jit(solution)/shard_map/all_to_all | solution.py:18
  103.3 24.1 %reduce-scatter.9.cloned.1.call-start = ((), (), s32[]{:S(2)}) async-start(), calls=%async_computation.10 | async-start | bytes 196608 | tf_op jit(solution)/shard_map/reduce_scatter | solution.py:149
  117.7 0.6 copy-start.7
  129.0 3.7 %copy-start.13 = (s32[1,2]{1,0:T(1,128)S(1)}, s32[1,2]{1,0:T(1,128)}, u32[]{:S(2)}) copy-start(s32[1,2]{1,0:T(1,128)} %param.29) | copy-start | bytes 28
  129.0 8.0 %all-to-all-start.3 = ((f32[2,1,64,256]{3,2,1,0:T(8,128)}), f32[2,1,64,256]{3,2,1,0:T(8,128)S(1)}, u32[]{:S(2)}, u32[]{:S(2)}) async-start(f32[2,1,64,256]{3,2,1,0:T(8,128)} %pad_maximum_fusion.3), calls=%async_computation.6 | async-start | bytes 262144 | tf_op jit(solution)/shard_map/all_to_all | solution.py:18
  132.5 31.1 %reduce-scatter.11.cloned.1.call-start = ((), (), s32[]{:S(2)}) async-start(), calls=%async_computation.11 | async-start | bytes 196608 | tf_op jit(solution)/shard_map/reduce_scatter | solution.py:149
  146.9 0.6 copy-start.8
  147.5 6.2 %copy-start.1 = (f32[4096]{0:T(1024)}, f32[4096]{0:T(1024)S(1)}, u32[]{:S(2)}) copy-start(f32[4096]{0:T(1024)S(1)} %fusion.130) | copy-start | bytes 49156
  153.8 19.2 %collective-permute-start.5 = (f32[2,512]{1,0:T(2,128)S(1)}, f32[2,512]{1,0:T(2,128)S(1)}, u32[]{:S(2)}, u32[]{:S(2)}) collective-permute-start(f32[2,512]{1,0:T(2,128)S(1)} %get-tuple-element.809), channel_id=1, source_target_pairs={{2,0},{4,2},{6,4},{8,6},{10,8},{12,10},{14,12},{16,14},{18,16},{20... | collective-permute-start | bytes 12296 | tf_op jit(solution)/shard_map/ppermute | solution.py:41
  159.4 13.6 %collective-permute-start.4 = (f32[2,512]{1,0:T(2,128)S(1)}, f32[2,512]{1,0:T(2,128)S(1)}, u32[]{:S(2)}, u32[]{:S(2)}) collective-permute-start(f32[2,512]{1,0:T(2,128)S(1)} %get-tuple-element.808), channel_id=1, source_target_pairs={{0,2},{2,4},{4,6},{6,8},{8,10},{10,12},{12,14},{14,16},{16,18},{18... | collective-permute-start | bytes 12296 | tf_op jit(solution)/shard_map/ppermute | solution.py:41
  164.5 9.2 %collective-permute-start.2 = (f32[1,64,256]{2,1,0:T(8,128)S(1)}, f32[1,64,256]{2,1,0:T(8,128)S(1)}, u32[]{:S(2)}, u32[]{:S(2)}) collective-permute-start(f32[1,64,256]{2,1,0:T(8,128)S(1)} %sub.161), channel_id=1, source_target_pairs={{1,0},{2,1},{3,2},{4,3},{5,4},{6,5},{7,6},{8,7},{9,8},{10,9},{11,1... | collective-permute-start | bytes 196616 | tf_op jit(solution)/shard_map/ppermute | solution.py:31
  171.1 9.8 %collective-permute-start.3 = (f32[1,64,256]{2,1,0:T(8,128)S(1)}, f32[1,64,256]{2,1,0:T(8,128)S(1)}, u32[]{:S(2)}, u32[]{:S(2)}) collective-permute-start(f32[1,64,256]{2,1,0:T(8,128)S(1)} %sub.161), channel_id=1, source_target_pairs={{0,1},{1,2},{2,3},{3,4},{4,5},{5,6},{6,7},{7,8},{8,9},{9,10},{10,1... | collective-permute-start | bytes 196616 | tf_op jit(solution)/shard_map/ppermute | solution.py:29
Sparse Core Ops, SparseCore 0:
  27.6 18.2 reduce-scatter.4
  65.9 15.8 reduce-scatter.6
  118.5 8.9 reduce-scatter.8
  147.7 15.9 reduce-scatter.10
